TPU v7x, 512 devices: a whole 4x4x16 slice. The times are simulated.
512 devices in a mesh: row: 32 (over z_lo, y, core), col: 16 (over x, z_hi).
Axes of the slice: x: 4, y: 4, z: 16 (z_hi: 4, z_lo: 4; z = z_hi * 4 + z_lo), core: 2. Of those that a mesh axis runs over, the one named last changes fastest.
Arguments:
- row_cells: int32 [3, 32768], P(None, 'row'), may hold values from 0 to 63
- col_cells: int32 [3, 131072], P(None, 'col'), may hold values from 0 to 63
- omega: float32 [16, 131072], P(None, 'col'), may hold values from -6 to 6
Outputs:
- basis: float32 [16, 32768], P(None, 'row')
- image: float32 [16, 131072], P(None, 'col')
- core: float32 [16, 16], replicated
All inputs are finite; a program needn't handle non-finite values.
Results may differ from a plain program's by a relative error of at most 0.0001.
Values sent between devices are 32-bit elements; how exact they have to be, the bound alone decides.
No kernel may reach another device: no remote copies, remote signals or barrier semaphores. Data moves between devices by JAX's collectives and lax.ppermute only.
A program may use at most 64 MiB of HBM per device.

v0:
```python
import jax
import jax.numpy as jnp
from jax import lax
from jax.sharding import Mesh
from jax.sharding import PartitionSpec as P

ROW = ("row_0", "row_1", "row_2")
COL = ("col_0", "col_1")
ROW_COL = ("row_0", "row_1", "row_2", "col_0", "col_1")


def sent_to_all(array, axis):
    copies = jnp.broadcast_to(array, (lax.axis_size(axis), *array.shape))
    return lax.all_to_all(copies, axis, split_axis=0, concat_axis=0, tiled=True)


def of_everyone(array, axis):
    return sent_to_all(array, axis).sum(axis=0)


def in_blocks(array, dim, length):
    before, after = (array.shape[:dim], array.shape[dim + 1 :])
    return jnp.moveaxis(array.reshape(*before, length, -1, *after), dim, 0)


def summed_on_arrival(array, axis, dim):
    parts = in_blocks(array, dim, lax.axis_size(axis))
    arrived = lax.all_to_all(parts, axis, split_axis=0, concat_axis=0, tiled=True)
    return arrived.sum(axis=0)


def over_axes(array, axes):
    for axis in axes:
        array = lax.psum(array, axis)
    return array


def joined_along(parts, dim):
    parts = jnp.moveaxis(parts, 0, dim)
    lengths = parts.shape
    return parts.reshape(*lengths[:dim], lengths[dim] * lengths[dim + 1], *lengths[dim + 2 :])


def gather_directly(array, axis, dim):
    return joined_along(sent_to_all(array, axis), dim)


def kernel_tile(rows, cols):
    first = (rows[0][:, None] - cols[0][None, :]).astype(jnp.float32)
    total = first * first
    second = (rows[1][:, None] - cols[1][None, :]).astype(jnp.float32)
    total = total + second * second
    third = (rows[2][:, None] - cols[2][None, :]).astype(jnp.float32)
    total = total + third * third
    return 0.25 * jnp.exp(-jnp.sqrt(total) / 6.4)


def shards(row_cells, col_cells, omega):
    rank = omega.shape[0]
    local_rows = row_cells.shape[1]
    local_cols = col_cells.shape[1]
    rows_total = local_rows * lax.axis_size(ROW)
    order = local_cols * lax.axis_size(COL)
    width = min(local_cols, 2048)
    count = local_cols // width

    def tile_at(index):
        cols = lax.dynamic_slice_in_dim(col_cells, index * width, width, 1)
        return kernel_tile(row_cells, cols)

    def sketch_step(index, total):
        tests = lax.dynamic_slice_in_dim(omega, index * width, width, 1)
        return total + lax.dot_general(
            tests, tile_at(index), (((1,), (1,)), ((), ())), precision=lax.Precision.HIGHEST
        )

    sketch_part = lax.fori_loop(0, count, sketch_step, jnp.zeros((rank, local_rows), jnp.float32))
    sketch = of_everyone(sketch_part, COL)
    gram = of_everyone(jnp.dot(sketch, sketch.T, precision=lax.Precision.HIGHEST), ROW) / rows_total
    lower = jnp.linalg.cholesky(gram)
    basis = jax.scipy.linalg.solve_triangular(lower, sketch, lower=True)

    def image_step(index, total):
        piece = jnp.dot(basis, tile_at(index), precision=lax.Precision.HIGHEST)
        return lax.dynamic_update_slice_in_dim(total, piece, index * width, 1)

    image_part = lax.fori_loop(0, count, image_step, jnp.zeros((rank, local_cols), jnp.float32))
    image_share = summed_on_arrival(image_part, ROW, 1)
    core = (
        over_axes(jnp.dot(image_share, image_share.T, precision=lax.Precision.HIGHEST), ROW_COL)
        / order
    )
    image = gather_directly(image_share, ROW, 1)
    return (basis, image, core)


def solution(mesh):
    finer = Mesh(mesh.devices.reshape(4, 4, 2, 4, 4), ("row_0", "row_1", "row_2", "col_0", "col_1"))
    return jax.shard_map(
        shards,
        mesh=finer,
        in_specs=(P(None, ROW), P(None, COL), P(None, COL)),
        out_specs=(P(None, ROW), P(None, COL), P()),
        check_vma=False,
    )
```

profile of v0, /device:TPU:64, one launch (start us, length us, event | category | flops | bytes accessed | tf_op | source)
XLA Modules:
  0.0 277.8 jit_solution(13617429852910083274)
XLA Ops:
  0.6 60.1 %while.28 = (s32[]{:T(128)}, f32[16,1024]{1,0:T(8,128)S(1)}, f32[16,8192]{1,0:T(8,128)}, s32[3,1024]{1,0:T(4,128)}, s32[3,8192]{1,0:T(4,128)}, /*index=5*/s32[]{...) while((s32[]{:T(128)}, f32[16,1024]{1,0:T(8,128)S(1)}, f32[16,8192]{1,0:T(8,128)}, ...), condition=%wide.region_1.0_spmd.clone, body=%wide.region_0.0_spmd.clone.sunk | while | flops 432046080 | bytes 372941 | solution.py:77
  0.7 1.0 constant_dynamic-slice_fusion.5
  1.6 0.8 fusion.93
  2.5 13.2 %fusion.94 = f32[16,1024]{1,0:T(8,128)S(1)} fusion(s32[2048]{0:T(1024)S(1)} %bitcast.72, s32[1024]{0:T(1024)S(1)} %bitcast.77, s32[2048]{0:T(1024)S(1)} %bitcast.71, s32[1024]{0:T(1024)S(1)} %bitcast.78, s32[2048]{0:T(1024)S(1)} %bitcast.70, s32[1024]{0:T(1024)S(1)} %bitcast.76, f32[16,8192]{1,0:T(8,128)} %get-tuple-element.353, s32[]{:T(128)S(6)} %select_n.28, ...), kind=kOutput, calls=%fused_computation.55.clone.1 | convolution fusion | flops 432046080 | bytes 299013 | tf_op jit(solution)/shard_map/while/body/eval_jaxpr/dot_general | solution.py:73
  15.7 1.0 constant_dynamic-slice_fusion.5
  16.7 0.8 fusion.93
  17.5 13.2 %fusion.94 = f32[16,1024]{1,0:T(8,128)S(1)} fusion(s32[2048]{0:T(1024)S(1)} %bitcast.72, s32[1024]{0:T(1024)S(1)} %bitcast.77, s32[2048]{0:T(1024)S(1)} %bitcast.71, s32[1024]{0:T(1024)S(1)} %bitcast.78, s32[2048]{0:T(1024)S(1)} %bitcast.70, s32[1024]{0:T(1024)S(1)} %bitcast.76, f32[16,8192]{1,0:T(8,128)} %get-tuple-element.353, s32[]{:T(128)S(6)} %select_n.28, ...), kind=kOutput, calls=%fused_computation.55.clone.1 | convolution fusion | flops 432046080 | bytes 299013 | tf_op jit(solution)/shard_map/while/body/eval_jaxpr/dot_general | solution.py:73
  30.7 1.0 constant_dynamic-slice_fusion.5
  31.7 0.8 fusion.93
  32.5 13.2 %fusion.94 = f32[16,1024]{1,0:T(8,128)S(1)} fusion(s32[2048]{0:T(1024)S(1)} %bitcast.72, s32[1024]{0:T(1024)S(1)} %bitcast.77, s32[2048]{0:T(1024)S(1)} %bitcast.71, s32[1024]{0:T(1024)S(1)} %bitcast.78, s32[2048]{0:T(1024)S(1)} %bitcast.70, s32[1024]{0:T(1024)S(1)} %bitcast.76, f32[16,8192]{1,0:T(8,128)} %get-tuple-element.353, s32[]{:T(128)S(6)} %select_n.28, ...), kind=kOutput, calls=%fused_computation.55.clone.1 | convolution fusion | flops 432046080 | bytes 299013 | tf_op jit(solution)/shard_map/while/body/eval_jaxpr/dot_general | solution.py:73
  45.7 1.0 constant_dynamic-slice_fusion.5
  46.7 0.8 fusion.93
  47.6 13.2 %fusion.94 = f32[16,1024]{1,0:T(8,128)S(1)} fusion(s32[2048]{0:T(1024)S(1)} %bitcast.72, s32[1024]{0:T(1024)S(1)} %bitcast.77, s32[2048]{0:T(1024)S(1)} %bitcast.71, s32[1024]{0:T(1024)S(1)} %bitcast.78, s32[2048]{0:T(1024)S(1)} %bitcast.70, s32[1024]{0:T(1024)S(1)} %bitcast.76, f32[16,8192]{1,0:T(8,128)} %get-tuple-element.353, s32[]{:T(128)S(6)} %select_n.28, ...), kind=kOutput, calls=%fused_computation.55.clone.1 | convolution fusion | flops 432046080 | bytes 299013 | tf_op jit(solution)/shard_map/while/body/eval_jaxpr/dot_general | solution.py:73
  60.9 71.5 %all_to_all.20 = f32[16,16,1024]{2,1,0:T(8,128)S(1)} all-to-all(f32[16,16,1024]{2,1,0:T(8,128)S(1)} %broadcast_in_dim.18), channel_id=1, replica_groups=mesh['row_0'=4,'row_1'=4,'row_2'=2,'col_0'=4,'col_1'=4] {'col_0','col_1'}, dimensions={0} | all-to-all | bytes 2097152 | tf_op jit(solution)/shard_map/all_to_all | solution.py:14
  132.5 0.2 fusion.71
  132.7 0.8 reshape.30
  133.5 8.5 %all-to-all-start.1 = ((f32[32,1,256]{2,1,0:T(1,128)}), f32[32,1,256]{2,1,0:T(1,128)S(1)}, u32[]{:S(2)}, u32[]{:S(2)}) async-start(f32[32,1,256]{2,1,0:T(1,128)} %reshape.30), calls=%async_computation.1 | async-start | bytes 65536 | tf_op jit(solution)/shard_map/all_to_all | solution.py:14
  142.0 5.7 %all-to-all-done.1 = f32[32,1,256]{2,1,0:T(1,128)S(1)} async-done(((f32[32,1,256]{2,1,0:T(1,128)}), f32[32,1,256]{2,1,0:T(1,128)S(1)}, u32[]{:S(2)}, u32[]{:S(2)}) %all-to-all-start.1) | async-done | bytes 32800 | tf_op jit(solution)/shard_map/all_to_all | solution.py:14
  147.7 0.5 broadcast.123
  148.2 0.7 reduce.6
  149.2 1.5 cholesky.16
  150.7 0.6 compare_reduce_fusion
  151.4 0.6 fusion.65
  152.0 1.2 custom-call.7
  153.2 0.3 fusion.66
  153.6 45.4 %while.27 = (s32[]{:T(128)}, f32[16,8192]{1,0:T(8,128)S(1)}, s32[3,1024]{1,0:T(4,128)S(1)}, s32[3,8192]{1,0:T(4,128)}, f32[16,1024]{1,0:T(8,128)S(1)}, /*index=5...) while((s32[]{:T(128)}, f32[16,8192]{1,0:T(8,128)S(1)}, s32[3,1024]{1,0:T(4,128)S(1)}, ...), condition=%wide.region_7.8_spmd, body=%wide.region_6.7_spmd.sunk | while | flops 432013312 | bytes 307395 | solution.py:87
  153.6 1.0 constant_dynamic-slice_fusion.4
  154.6 10.3 %fusion.90 = f32[16,8192]{1,0:T(8,128)S(1)} fusion(f32[16,8192]{1,0:T(8,128)S(1)} %get-tuple-element.374, s32[]{:T(128)S(6)} %select_n.27, f32[16,1024]{1,0:T(8,128)S(1)} %get-tuple-element.388, s32[2048]{0:T(1024)S(1)} %bitcast.75, s32[1024]{0:T(1024)S(1)} %bitcast.80, s32[2048]{0:T(1024)S(1)} %bitcast.74, s32[1024]{0:T(1024)S(1)} %bitcast.81, ...), kind=kOutput, calls=%fused_computation.26.clone.1 | convolution fusion | flops 432013312 | bytes 233476 | tf_op jit(solution)/shard_map/while/body/eval_jaxpr/dot_general | solution.py:84
  164.9 1.0 constant_dynamic-slice_fusion.4
  165.9 10.3 %fusion.90 = f32[16,8192]{1,0:T(8,128)S(1)} fusion(f32[16,8192]{1,0:T(8,128)S(1)} %get-tuple-element.374, s32[]{:T(128)S(6)} %select_n.27, f32[16,1024]{1,0:T(8,128)S(1)} %get-tuple-element.388, s32[2048]{0:T(1024)S(1)} %bitcast.75, s32[1024]{0:T(1024)S(1)} %bitcast.80, s32[2048]{0:T(1024)S(1)} %bitcast.74, s32[1024]{0:T(1024)S(1)} %bitcast.81, ...), kind=kOutput, calls=%fused_computation.26.clone.1 | convolution fusion | flops 432013312 | bytes 233476 | tf_op jit(solution)/shard_map/while/body/eval_jaxpr/dot_general | solution.py:84
  176.3 1.0 constant_dynamic-slice_fusion.4
  177.3 10.3 %fusion.90 = f32[16,8192]{1,0:T(8,128)S(1)} fusion(f32[16,8192]{1,0:T(8,128)S(1)} %get-tuple-element.374, s32[]{:T(128)S(6)} %select_n.27, f32[16,1024]{1,0:T(8,128)S(1)} %get-tuple-element.388, s32[2048]{0:T(1024)S(1)} %bitcast.75, s32[1024]{0:T(1024)S(1)} %bitcast.80, s32[2048]{0:T(1024)S(1)} %bitcast.74, s32[1024]{0:T(1024)S(1)} %bitcast.81, ...), kind=kOutput, calls=%fused_computation.26.clone.1 | convolution fusion | flops 432013312 | bytes 233476 | tf_op jit(solution)/shard_map/while/body/eval_jaxpr/dot_general | solution.py:84
  187.6 1.0 constant_dynamic-slice_fusion.4
  188.6 10.3 %fusion.90 = f32[16,8192]{1,0:T(8,128)S(1)} fusion(f32[16,8192]{1,0:T(8,128)S(1)} %get-tuple-element.374, s32[]{:T(128)S(6)} %select_n.27, f32[16,1024]{1,0:T(8,128)S(1)} %get-tuple-element.388, s32[2048]{0:T(1024)S(1)} %bitcast.75, s32[1024]{0:T(1024)S(1)} %bitcast.80, s32[2048]{0:T(1024)S(1)} %bitcast.74, s32[1024]{0:T(1024)S(1)} %bitcast.81, ...), kind=kOutput, calls=%fused_computation.26.clone.1 | convolution fusion | flops 432013312 | bytes 233476 | tf_op jit(solution)/shard_map/while/body/eval_jaxpr/dot_general | solution.py:84
  199.0 0.2 copy.20
  199.1 0.3 copy.16
  199.4 0.1 copy-done.1
  199.6 19.7 %all_to_all.21 = f32[32,16,256]{2,1,0:T(8,128)S(1)} all-to-all(f32[32,16,256]{2,1,0:T(8,128)S(1)} %copy.16), channel_id=1, replica_groups=mesh['row_0'=4,'row_1'=4,'row_2'=2,'col_0'=4,'col_1'=4] {'row_0','row_1'..., dimensions={0} | all-to-all | bytes 1048576 | tf_op jit(solution)/shard_map/all_to_all | solution.py:28
  219.3 0.9 broadcast_in_dim.21
  220.2 5.8 %all-to-all-start.3 = ((f32[32,16,256]{2,1,0:T(8,128)}), f32[32,16,256]{2,1,0:T(8,128)S(1)}, u32[]{:S(2)}, u32[]{:S(2)}) async-start(f32[32,16,256]{2,1,0:T(8,128)} %broadcast_in_dim.21), calls=%async_computation.3 | async-start | bytes 1048576 | tf_op jit(solution)/shard_map/all_to_all | solution.py:14
  226.0 0.1 fusion.72
  226.1 16.3 %psum.35 = f32[16,16]{1,0:T(8,128)S(1)} all-reduce(f32[16,16]{1,0:T(8,128)S(1)} %fusion.72), channel_id=1, replica_groups=mesh['row_0'=4,'row_1'=4,'row_2'=2,'col_0'=4,'col_1'=4] {'row_0'}, use_global_device_ids=true, to_apply=%region_9.10 | all-reduce | flops 256 | bytes 2048 | tf_op jit(solution)/shard_map/psum | solution.py:34
  242.5 10.5 %psum.36 = f32[16,16]{1,0:T(8,128)S(1)} all-reduce(f32[16,16]{1,0:T(8,128)S(1)} %psum.35), channel_id=1, replica_groups=mesh['row_0'=4,'row_1'=4,'row_2'=2,'col_0'=4,'col_1'=4] {'row_1'}, use_global_device_ids=true, to_apply=%region_10.11 | all-reduce | flops 256 | bytes 2048 | tf_op jit(solution)/shard_map/psum | solution.py:34
  253.0 2.5 psum.37
  255.5 8.7 %psum.38 = f32[16,16]{1,0:T(8,128)S(1)} all-reduce(f32[16,16]{1,0:T(8,128)S(1)} %psum.37), channel_id=1, replica_groups=mesh['row_0'=4,'row_1'=4,'row_2'=2,'col_0'=4,'col_1'=4] {'col_0'}, use_global_device_ids=true, to_apply=%region_12.13 | all-reduce | flops 256 | bytes 2048 | tf_op jit(solution)/shard_map/psum | solution.py:34
  264.2 12.1 %psum.39 = f32[16,16]{1,0:T(8,128)S(1)} all-reduce(f32[16,16]{1,0:T(8,128)S(1)} %psum.38), channel_id=1, replica_groups=mesh['row_0'=4,'row_1'=4,'row_2'=2,'col_0'=4,'col_1'=4] {'col_1'}, use_global_device_ids=true, to_apply=%region_13.14 | all-reduce | flops 256 | bytes 2048 | tf_op jit(solution)/shard_map/psum | solution.py:34
  276.4 0.6 broadcast_multiply_fusion
  277.0 0.8 copy.19
  (19 shorter events, 0.6 us)
Async XLA Ops:
  132.5 21.1 %copy-start = (s32[3,1024]{1,0:T(4,128)S(1)}, s32[3,1024]{1,0:T(4,128)}, u32[]{:S(2)}) copy-start(s32[3,1024]{1,0:T(4,128)} %get-tuple-element.396) | copy-start | bytes 36868
  133.5 14.3 %all-to-all-start.1 = ((f32[32,1,256]{2,1,0:T(1,128)}), f32[32,1,256]{2,1,0:T(1,128)S(1)}, u32[]{:S(2)}, u32[]{:S(2)}) async-start(f32[32,1,256]{2,1,0:T(1,128)} %reshape.30), calls=%async_computation.1 | async-start | bytes 65536 | tf_op jit(solution)/shard_map/all_to_all | solution.py:14
  199.0 0.6 copy-start.1
  220.2 56.8 %all-to-all-start.3 = ((f32[32,16,256]{2,1,0:T(8,128)}), f32[32,16,256]{2,1,0:T(8,128)S(1)}, u32[]{:S(2)}, u32[]{:S(2)}) async-start(f32[32,16,256]{2,1,0:T(8,128)} %broadcast_in_dim.21), calls=%async_computation.3 | async-start | bytes 1048576 | tf_op jit(solution)/shard_map/all_to_all | solution.py:14
where the time goes:
time: 279 us; the launch traced here: 278 us
  blocking collectives  141 us (51%)
  matrix products  94.5 us (34%)
  local copies, waits for them, and re-layouts  15.2 us (5%)
  starting transfers between devices  14.4 us (5%)
  waiting for transfers between devices  5.72 us (2%)
  other arithmetic  5.48 us (2%)
    all_to_all x1, blocking collectives, sent_to_all(): return lax.all_to_all(copies, axis, split_axis=0, concat_axis=0, tiled=True)  71.5 us
    dot_general x4, matrix products, sketch_step(): lax.dot_general(tests, tile_at(index), (((1,), (1,)), ((), ())), precisio...  52.6 us
    psum x5, blocking collectives, over_axes(): array = lax.psum(array, axis)  50.2 us
    dot_general x4, matrix products, image_step(): piece = jnp.dot(basis, tile_at(index), precision=lax.Precision.HIGHEST)  41.3 us
    all_to_all x1, blocking collectives, summed_on_arrival(): lax.all_to_all(parts, axis, split_axis=0, concat_axis=0, tiled=True)  19.7 us
    all_to_all x2, starting transfers between devices, sent_to_all(): return lax.all_to_all(copies, axis, split_axis=0, concat_axis=0, tiled=True)  14.4 us
    slice x16, local copies, waits for them, and re-layouts, kernel_tile(): first = (rows[0][:, None] - cols[0][None, :]).astype(jnp.float32)  11.2 us
    all_to_all x2, waiting for transfers between devices, sent_to_all(): return lax.all_to_all(copies, axis, split_axis=0, concat_axis=0, tiled=True)  5.72 us
  transfers between devices with their start and end apart: 2, of which 1 were waited for; matrix products, arithmetic and copies ran while one was open for 0% of the time, Pallas kernels for 0%

commit v1 on v0

--- a/solution.py
+++ b/solution.py
@@ -31,7 +31,7 @@
 
 def over_axes(array, axes):
     for axis in axes:
-        array = lax.psum(array, axis)
+        array = jnp.sum(lax.all_gather(array, axis), axis=0)
     return array
 
 

time: 279 us -> 293 us (1.050)
  the two profiles are of different devices: /device:TPU:64 before, /device:TPU:8 now
where the time goes in v1:
time: 293 us; the launch traced here: 291 us
  blocking collectives  156 us (53%)
  matrix products  94.5 us (32%)
  local copies, waits for them, and re-layouts  15.2 us (5%)
  starting transfers between devices  12.4 us (4%)
  waiting for transfers between devices  6.57 us (2%)
  other arithmetic  5.52 us (2%)
    all_to_all x1, blocking collectives, sent_to_all(): return lax.all_to_all(copies, axis, split_axis=0, concat_axis=0, tiled=True)  74.2 us
    all_gather x5, blocking collectives, over_axes(): array = jnp.sum(lax.all_gather(array, axis), axis=0)  63 us
    dot_general x4, matrix products, sketch_step(): lax.dot_general(tests, tile_at(index), (((1,), (1,)), ((), ())), precisio...  52.6 us
    dot_general x4, matrix products, image_step(): piece = jnp.dot(basis, tile_at(index), precision=lax.Precision.HIGHEST)  41.3 us
    all_to_all x1, blocking collectives, summed_on_arrival(): lax.all_to_all(parts, axis, split_axis=0, concat_axis=0, tiled=True)  18.9 us
    all_to_all x2, starting transfers between devices, sent_to_all(): return lax.all_to_all(copies, axis, split_axis=0, concat_axis=0, tiled=True)  12.4 us
    slice x16, local copies, waits for them, and re-layouts, kernel_tile(): first = (rows[0][:, None] - cols[0][None, :]).astype(jnp.float32)  11.2 us
    all_to_all x2, waiting for transfers between devices, sent_to_all(): return lax.all_to_all(copies, axis, split_axis=0, concat_axis=0, tiled=True)  6.57 us
  transfers between devices with their start and end apart: 2, of which 1 were waited for; matrix products, arithmetic and copies ran while one was open for 0% of the time, Pallas kernels for 0%

profile of v1, /device:TPU:8, one launch (start us, length us, event | category | flops | bytes accessed | tf_op | source)
XLA Modules:
  0.0 291.4 jit_solution(8758859111663888131)
XLA Ops:
  0.6 60.1 %while.28 = (s32[]{:T(128)}, f32[16,1024]{1,0:T(8,128)S(1)}, f32[16,8192]{1,0:T(8,128)}, s32[3,1024]{1,0:T(4,128)}, s32[3,8192]{1,0:T(4,128)}, /*index=5*/s32[]{...) while((s32[]{:T(128)}, f32[16,1024]{1,0:T(8,128)S(1)}, f32[16,8192]{1,0:T(8,128)}, ...), condition=%wide.region_1.0_spmd.clone, body=%wide.region_0.0_spmd.clone.sunk | while | flops 432046080 | bytes 372941 | solution.py:77
  0.7 1.0 constant_dynamic-slice_fusion.5
  1.6 0.8 fusion.93
  2.5 13.2 %fusion.94 = f32[16,1024]{1,0:T(8,128)S(1)} fusion(s32[2048]{0:T(1024)S(1)} %bitcast.77, s32[1024]{0:T(1024)S(1)} %bitcast.86, s32[2048]{0:T(1024)S(1)} %bitcast.76, s32[1024]{0:T(1024)S(1)} %bitcast.87, s32[2048]{0:T(1024)S(1)} %bitcast.75, s32[1024]{0:T(1024)S(1)} %bitcast.85, f32[16,8192]{1,0:T(8,128)} %get-tuple-element.353, s32[]{:T(128)S(6)} %select_n.28, ...), kind=kOutput, calls=%fused_computation.55.clone.1 | convolution fusion | flops 432046080 | bytes 299013 | tf_op jit(solution)/shard_map/while/body/eval_jaxpr/dot_general | solution.py:73
  15.7 1.0 constant_dynamic-slice_fusion.5
  16.7 0.8 fusion.93
  17.5 13.2 %fusion.94 = f32[16,1024]{1,0:T(8,128)S(1)} fusion(s32[2048]{0:T(1024)S(1)} %bitcast.77, s32[1024]{0:T(1024)S(1)} %bitcast.86, s32[2048]{0:T(1024)S(1)} %bitcast.76, s32[1024]{0:T(1024)S(1)} %bitcast.87, s32[2048]{0:T(1024)S(1)} %bitcast.75, s32[1024]{0:T(1024)S(1)} %bitcast.85, f32[16,8192]{1,0:T(8,128)} %get-tuple-element.353, s32[]{:T(128)S(6)} %select_n.28, ...), kind=kOutput, calls=%fused_computation.55.clone.1 | convolution fusion | flops 432046080 | bytes 299013 | tf_op jit(solution)/shard_map/while/body/eval_jaxpr/dot_general | solution.py:73
  30.7 1.0 constant_dynamic-slice_fusion.5
  31.7 0.8 fusion.93
  32.5 13.2 %fusion.94 = f32[16,1024]{1,0:T(8,128)S(1)} fusion(s32[2048]{0:T(1024)S(1)} %bitcast.77, s32[1024]{0:T(1024)S(1)} %bitcast.86, s32[2048]{0:T(1024)S(1)} %bitcast.76, s32[1024]{0:T(1024)S(1)} %bitcast.87, s32[2048]{0:T(1024)S(1)} %bitcast.75, s32[1024]{0:T(1024)S(1)} %bitcast.85, f32[16,8192]{1,0:T(8,128)} %get-tuple-element.353, s32[]{:T(128)S(6)} %select_n.28, ...), kind=kOutput, calls=%fused_computation.55.clone.1 | convolution fusion | flops 432046080 | bytes 299013 | tf_op jit(solution)/shard_map/while/body/eval_jaxpr/dot_general | solution.py:73
  45.7 1.0 constant_dynamic-slice_fusion.5
  46.7 0.8 fusion.93
  47.6 13.2 %fusion.94 = f32[16,1024]{1,0:T(8,128)S(1)} fusion(s32[2048]{0:T(1024)S(1)} %bitcast.77, s32[1024]{0:T(1024)S(1)} %bitcast.86, s32[2048]{0:T(1024)S(1)} %bitcast.76, s32[1024]{0:T(1024)S(1)} %bitcast.87, s32[2048]{0:T(1024)S(1)} %bitcast.75, s32[1024]{0:T(1024)S(1)} %bitcast.85, f32[16,8192]{1,0:T(8,128)} %get-tuple-element.353, s32[]{:T(128)S(6)} %select_n.28, ...), kind=kOutput, calls=%fused_computation.55.clone.1 | convolution fusion | flops 432046080 | bytes 299013 | tf_op jit(solution)/shard_map/while/body/eval_jaxpr/dot_general | solution.py:73
  60.9 74.2 %all_to_all.20 = f32[16,16,1024]{2,1,0:T(8,128)S(1)} all-to-all(f32[16,16,1024]{2,1,0:T(8,128)S(1)} %broadcast_in_dim.18), channel_id=1, replica_groups=mesh['row_0'=4,'row_1'=4,'row_2'=2,'col_0'=4,'col_1'=4] {'col_0','col_1'}, dimensions={0} | all-to-all | bytes 2097152 | tf_op jit(solution)/shard_map/all_to_all | solution.py:14
  135.1 0.2 fusion.71
  135.4 0.8 reshape.35
  136.1 6.7 %all-to-all-start.1 = ((f32[32,1,256]{2,1,0:T(1,128)}), f32[32,1,256]{2,1,0:T(1,128)S(1)}, u32[]{:S(2)}, u32[]{:S(2)}) async-start(f32[32,1,256]{2,1,0:T(1,128)} %reshape.35), calls=%async_computation.1 | async-start | bytes 65536 | tf_op jit(solution)/shard_map/all_to_all | solution.py:14
  142.8 6.6 %all-to-all-done.1 = f32[32,1,256]{2,1,0:T(1,128)S(1)} async-done(((f32[32,1,256]{2,1,0:T(1,128)}), f32[32,1,256]{2,1,0:T(1,128)S(1)}, u32[]{:S(2)}, u32[]{:S(2)}) %all-to-all-start.1) | async-done | bytes 32800 | tf_op jit(solution)/shard_map/all_to_all | solution.py:14
  149.4 0.5 broadcast.123
  149.9 0.7 reduce.6
  150.9 1.5 cholesky.16
  152.4 0.6 compare_reduce_fusion
  153.0 0.6 fusion.65
  153.7 1.2 custom-call.7
  154.9 0.3 fusion.66
  155.2 45.4 %while.27 = (s32[]{:T(128)}, f32[16,8192]{1,0:T(8,128)S(1)}, s32[3,1024]{1,0:T(4,128)S(1)}, s32[3,8192]{1,0:T(4,128)}, f32[16,1024]{1,0:T(8,128)S(1)}, /*index=5...) while((s32[]{:T(128)}, f32[16,8192]{1,0:T(8,128)S(1)}, s32[3,1024]{1,0:T(4,128)S(1)}, ...), condition=%wide.region_7.8_spmd, body=%wide.region_6.7_spmd.sunk | while | flops 432013312 | bytes 307395 | solution.py:87
  155.2 1.0 constant_dynamic-slice_fusion.4
  156.2 10.3 %fusion.90 = f32[16,8192]{1,0:T(8,128)S(1)} fusion(f32[16,8192]{1,0:T(8,128)S(1)} %get-tuple-element.374, s32[]{:T(128)S(6)} %select_n.27, f32[16,1024]{1,0:T(8,128)S(1)} %get-tuple-element.388, s32[2048]{0:T(1024)S(1)} %bitcast.80, s32[1024]{0:T(1024)S(1)} %bitcast.89, s32[2048]{0:T(1024)S(1)} %bitcast.79, s32[1024]{0:T(1024)S(1)} %bitcast.90, ...), kind=kOutput, calls=%fused_computation.26.clone.1 | convolution fusion | flops 432013312 | bytes 233476 | tf_op jit(solution)/shard_map/while/body/eval_jaxpr/dot_general | solution.py:84
  166.6 1.0 constant_dynamic-slice_fusion.4
  167.6 10.3 %fusion.90 = f32[16,8192]{1,0:T(8,128)S(1)} fusion(f32[16,8192]{1,0:T(8,128)S(1)} %get-tuple-element.374, s32[]{:T(128)S(6)} %select_n.27, f32[16,1024]{1,0:T(8,128)S(1)} %get-tuple-element.388, s32[2048]{0:T(1024)S(1)} %bitcast.80, s32[1024]{0:T(1024)S(1)} %bitcast.89, s32[2048]{0:T(1024)S(1)} %bitcast.79, s32[1024]{0:T(1024)S(1)} %bitcast.90, ...), kind=kOutput, calls=%fused_computation.26.clone.1 | convolution fusion | flops 432013312 | bytes 233476 | tf_op jit(solution)/shard_map/while/body/eval_jaxpr/dot_general | solution.py:84
  177.9 1.0 constant_dynamic-slice_fusion.4
  178.9 10.3 %fusion.90 = f32[16,8192]{1,0:T(8,128)S(1)} fusion(f32[16,8192]{1,0:T(8,128)S(1)} %get-tuple-element.374, s32[]{:T(128)S(6)} %select_n.27, f32[16,1024]{1,0:T(8,128)S(1)} %get-tuple-element.388, s32[2048]{0:T(1024)S(1)} %bitcast.80, s32[1024]{0:T(1024)S(1)} %bitcast.89, s32[2048]{0:T(1024)S(1)} %bitcast.79, s32[1024]{0:T(1024)S(1)} %bitcast.90, ...), kind=kOutput, calls=%fused_computation.26.clone.1 | convolution fusion | flops 432013312 | bytes 233476 | tf_op jit(solution)/shard_map/while/body/eval_jaxpr/dot_general | solution.py:84
  189.3 1.0 constant_dynamic-slice_fusion.4
  190.3 10.3 %fusion.90 = f32[16,8192]{1,0:T(8,128)S(1)} fusion(f32[16,8192]{1,0:T(8,128)S(1)} %get-tuple-element.374, s32[]{:T(128)S(6)} %select_n.27, f32[16,1024]{1,0:T(8,128)S(1)} %get-tuple-element.388, s32[2048]{0:T(1024)S(1)} %bitcast.80, s32[1024]{0:T(1024)S(1)} %bitcast.89, s32[2048]{0:T(1024)S(1)} %bitcast.79, s32[1024]{0:T(1024)S(1)} %bitcast.90, ...), kind=kOutput, calls=%fused_computation.26.clone.1 | convolution fusion | flops 432013312 | bytes 233476 | tf_op jit(solution)/shard_map/while/body/eval_jaxpr/dot_general | solution.py:84
  200.6 0.2 copy.20
  200.8 0.3 copy.16
  201.1 0.1 copy-done.1
  201.2 18.9 %all_to_all.21 = f32[32,16,256]{2,1,0:T(8,128)S(1)} all-to-all(f32[32,16,256]{2,1,0:T(8,128)S(1)} %copy.16), channel_id=1, replica_groups=mesh['row_0'=4,'row_1'=4,'row_2'=2,'col_0'=4,'col_1'=4] {'row_0','row_1'..., dimensions={0} | all-to-all | bytes 1048576 | tf_op jit(solution)/shard_map/all_to_all | solution.py:28
  220.2 0.9 broadcast_in_dim.21
  221.0 5.8 %all-to-all-start.3 = ((f32[32,16,256]{2,1,0:T(8,128)}), f32[32,16,256]{2,1,0:T(8,128)S(1)}, u32[]{:S(2)}, u32[]{:S(2)}) async-start(f32[32,16,256]{2,1,0:T(8,128)} %broadcast_in_dim.21), calls=%async_computation.3 | async-start | bytes 1048576 | tf_op jit(solution)/shard_map/all_to_all | solution.py:14
  226.8 0.1 fusion.72
  226.9 20.0 %all-gather = f32[64,16]{1,0:T(8,128)S(1)} all-gather(f32[16,16]{1,0:T(8,128)S(1)} %fusion.72), channel_id=2, replica_groups=mesh['row_0'=4,'row_1'=4,'row_2'=2,'col_0'=4,'col_1'=4] {'row_0'}, dimensions={0}, use_global_device_ids=true | all-gather | bytes 5120 | tf_op jit(solution)/shard_map/all_gather | solution.py:34
  246.9 11.9 %all-gather.1 = f32[64,16]{1,0:T(8,128)S(1)} all-gather(f32[16,16]{1,0:T(8,128)S(1)} %reduce_sum.78), channel_id=3, replica_groups=mesh['row_0'=4,'row_1'=4,'row_2'=2,'col_0'=4,'col_1'=4] {'row_1'}, dimensions={0}, use_global_device_ids=true | all-gather | bytes 5120 | tf_op jit(solution)/shard_map/all_gather | solution.py:34
  258.9 1.8 all-gather.2
  260.7 11.9 %all-gather.3 = f32[64,16]{1,0:T(8,128)S(1)} all-gather(f32[16,16]{1,0:T(8,128)S(1)} %reduce_sum.80), channel_id=5, replica_groups=mesh['row_0'=4,'row_1'=4,'row_2'=2,'col_0'=4,'col_1'=4] {'col_0'}, dimensions={0}, use_global_device_ids=true | all-gather | bytes 5120 | tf_op jit(solution)/shard_map/all_gather | solution.py:34
  272.6 17.3 %all-gather.4 = f32[64,16]{1,0:T(8,128)S(1)} all-gather(f32[16,16]{1,0:T(8,128)S(1)} %reduce_sum.81), channel_id=6, replica_groups=mesh['row_0'=4,'row_1'=4,'row_2'=2,'col_0'=4,'col_1'=4] {'col_1'}, dimensions={0}, use_global_device_ids=true | all-gather | bytes 5120 | tf_op jit(solution)/shard_map/all_gather | solution.py:34
  289.9 0.6 broadcast_multiply_fusion
  290.5 0.8 copy.19
  (24 shorter events, 0.7 us)
Async XLA Ops:
  135.1 20.1 %copy-start = (s32[3,1024]{1,0:T(4,128)S(1)}, s32[3,1024]{1,0:T(4,128)}, u32[]{:S(2)}) copy-start(s32[3,1024]{1,0:T(4,128)} %get-tuple-element.396) | copy-start | bytes 36868
  136.1 13.3 %all-to-all-start.1 = ((f32[32,1,256]{2,1,0:T(1,128)}), f32[32,1,256]{2,1,0:T(1,128)S(1)}, u32[]{:S(2)}, u32[]{:S(2)}) async-start(f32[32,1,256]{2,1,0:T(1,128)} %reshape.35), calls=%async_computation.1 | async-start | bytes 65536 | tf_op jit(solution)/shard_map/all_to_all | solution.py:14
  200.6 0.6 copy-start.1
  221.0 69.5 %all-to-all-start.3 = ((f32[32,16,256]{2,1,0:T(8,128)}), f32[32,16,256]{2,1,0:T(8,128)S(1)}, u32[]{:S(2)}, u32[]{:S(2)}) async-start(f32[32,16,256]{2,1,0:T(8,128)} %broadcast_in_dim.21), calls=%async_computation.3 | async-start | bytes 1048576 | tf_op jit(solution)/shard_map/all_to_all | solution.py:14
